TPU v7x, 128 devices: a whole 4x4x4 slice. The times are simulated.
128 devices in a mesh: row: 16 (over y, z_lo, core), col: 8 (over z_hi, x).
Axes of the slice: x: 4, y: 4, z: 4 (z_hi: 2, z_lo: 2; z = z_hi * 2 + z_lo), core: 2. Of those that a mesh axis runs over, the one named last changes fastest.
Arguments:
- z_trunk: bfloat16 [1024, 1024, 128], P('row', 'col'), may hold values from -6 to 6
- coords: int32 [3, 1024], P(None, ('row', 'col')), may hold values from 0 to 255
- token_mask: int32 [1024], P(('row', 'col')), may hold values 0 or 1
- w_dist: bfloat16 [39, 128], replicated, may hold values from -6 to 6
- w_attn: bfloat16 [128, 512], replicated, may hold values from -0.5 to 0.5
- w_bias: bfloat16 [128, 4], replicated, may hold values from -100 to 100
- w_out: bfloat16 [128, 128], replicated, may hold values from -2 to 2
- w_pae: bfloat16 [128, 64], replicated, may hold values from -0.5 to 0.5
- w_pde: bfloat16 [128, 64], replicated, may hold values from -0.5 to 0.5
Outputs:
- logits: float32 [1024, 1024, 128], P('row', 'col')
All inputs are finite; a program needn't handle non-finite values. No bound on the sum of `token_mask` on one device may be relied on, other than what follows from the above.
Results may differ from a plain program's by a relative error of at most 0.0055.
The roundings to bfloat16 on the way count: a program that leaves them out, or rounds other values in their place, can miss the bound.
Values may be sent and summed in bfloat16 or wider, within the bound.
A program may use at most 192 MiB of HBM per device.

v0:
```python
import jax
import jax.numpy as jnp
from jax import lax
from jax.sharding import PartitionSpec as P


def layer_norm(values):
    widened = values.astype(jnp.float32)
    average = jnp.mean(widened, axis=-1, keepdims=True)
    centred = widened - average
    variance = jnp.mean(centred * centred, axis=-1, keepdims=True)
    return (centred * lax.rsqrt(variance + 1e-05)).astype(jnp.bfloat16)


def distance_bins(coord_rows, coord_cols, class_count):
    offsets = coord_rows[:, :, None] - coord_cols[:, None, :]
    squared = jnp.sum(offsets * offsets, axis=0)
    bin_edges = 27 + 4 * jnp.arange(class_count - 1, dtype=jnp.int32)
    above = (squared[:, :, None] > (bin_edges * bin_edges)[None, None, :]).astype(jnp.int32)
    return jnp.sum(above, axis=-1)


def attend_column(query_rows, key_rows, value_rows, bias_full, key_bias):
    length_all = query_rows.shape[0]
    block_rows = min(512, length_all)

    def one_block(first_row):
        query_block = lax.dynamic_slice_in_dim(query_rows, first_row, block_rows, 0)
        bias_block = lax.dynamic_slice_in_dim(bias_full, first_row, block_rows, 2)
        scores = jnp.einsum(
            "khd,ihd->hki", key_rows, query_block, preferred_element_type=jnp.float32
        )
        scores = scores + bias_block + key_bias[None, :, None]
        highest = jnp.max(scores, axis=1, keepdims=True)
        raised = jnp.exp(scores - highest)
        weights = (raised / jnp.sum(raised, axis=1, keepdims=True)).astype(jnp.bfloat16)
        return jnp.einsum("hki,khd->ihd", weights, value_rows, preferred_element_type=jnp.float32)

    starts = jnp.arange(length_all // block_rows, dtype=jnp.int32) * block_rows
    blocks_out = lax.map(one_block, starts)
    return blocks_out.reshape(length_all, query_rows.shape[1], query_rows.shape[2])


def error_logits(updated, mirrored, w_pae, w_pde):
    width = updated.shape[-1]
    symmetric = updated.astype(jnp.float32) + mirrored.astype(jnp.float32)
    pae_part = jnp.dot(
        layer_norm(updated).reshape(-1, width), w_pae, preferred_element_type=jnp.float32
    )
    pde_part = jnp.dot(
        layer_norm(symmetric).reshape(-1, width), w_pde, preferred_element_type=jnp.float32
    )
    return jnp.concatenate([pae_part, pde_part], axis=1).reshape(
        updated.shape[0], updated.shape[1], -1
    )


def per_device(z_trunk, coords, token_mask, w_dist, w_attn, w_bias, w_out, w_pae, w_pde):
    all_coords, all_mask = (
        lax.all_gather(coords, ("row", "col"), axis=1, tiled=True),
        lax.all_gather(token_mask, ("row", "col"), axis=0, tiled=True),
    )
    rows_dev = z_trunk.shape[0]
    cols_dev = z_trunk.shape[1]
    width = z_trunk.shape[2]
    n_rows = lax.axis_size("row")
    n_cols = lax.axis_size("col")
    total = rows_dev * n_rows
    slab = rows_dev // n_cols
    heads = w_bias.shape[1]
    head_dim = width // heads
    classes = w_dist.shape[0]
    row_first = lax.axis_index("row") * rows_dev
    col_first = lax.axis_index("col") * cols_dev
    coord_rows = lax.dynamic_slice_in_dim(all_coords, row_first, rows_dev, 1)
    coord_cols = lax.dynamic_slice_in_dim(all_coords, col_first, cols_dev, 1)
    bins_tile = distance_bins(coord_rows, coord_cols, classes)
    one_hot = (bins_tile[:, :, None] == jnp.arange(classes, dtype=jnp.int32)[None, None, :]).astype(
        jnp.bfloat16
    )
    embedded = jnp.dot(one_hot.reshape(-1, classes), w_dist, preferred_element_type=jnp.float32)
    pair = (z_trunk.astype(jnp.float32) + embedded.reshape(rows_dev, cols_dev, width)).astype(
        jnp.bfloat16
    )
    pair_cols = lax.all_to_all(pair, "row", split_axis=1, concat_axis=0, tiled=True)
    normed = layer_norm(pair_cols)
    flat_normed = normed.reshape(-1, width)
    projected = jnp.dot(flat_normed, w_attn, preferred_element_type=jnp.float32)
    query_all = (
        (projected[:, :width] * head_dim ** (-0.5))
        .astype(jnp.bfloat16)
        .reshape(total, slab, heads, head_dim)
    )
    key_all = (
        projected[:, width : 2 * width].astype(jnp.bfloat16).reshape(total, slab, heads, head_dim)
    )
    value_all = (
        projected[:, 2 * width : 3 * width]
        .astype(jnp.bfloat16)
        .reshape(total, slab, heads, head_dim)
    )
    gate_all = projected[:, 3 * width :].astype(jnp.bfloat16)
    bias_local = jnp.einsum("kic,ch->hki", normed, w_bias, preferred_element_type=jnp.float32)
    gathered = lax.all_gather(bias_local, ("row", "col"), axis=2, tiled=True)
    bias_full = (
        gathered.reshape(heads, total, n_rows, n_cols, slab)
        .transpose(0, 1, 3, 2, 4)
        .reshape(heads, total, total)
    )
    key_bias = (all_mask.astype(jnp.float32) - 1.0) * 30000.0

    def one_column(operands):
        query_rows, key_rows, value_rows = operands
        return attend_column(query_rows, key_rows, value_rows, bias_full, key_bias)

    attended = lax.map(
        one_column,
        (jnp.swapaxes(query_all, 0, 1), jnp.swapaxes(key_all, 0, 1), jnp.swapaxes(value_all, 0, 1)),
    )
    attended = jnp.swapaxes(attended, 0, 1).reshape(total * slab, width)
    gated = (jax.nn.sigmoid(gate_all.astype(jnp.float32)) * attended).astype(jnp.bfloat16)
    update = jnp.dot(gated, w_out, preferred_element_type=jnp.float32)
    updated = (pair_cols.reshape(-1, width).astype(jnp.float32) + update).astype(jnp.bfloat16)
    updated = updated.reshape(total, slab, width)
    pieces = updated.reshape(n_cols, n_rows, slab, slab, width).transpose(1, 0, 2, 3, 4)
    flat_pieces = pieces.reshape(n_rows * n_cols, slab, slab, width)
    moved = lax.all_to_all(flat_pieces, ("row", "col"), split_axis=0, concat_axis=0, tiled=True)
    moved = moved.reshape(n_rows, n_cols, slab, slab, width)
    mirrored = moved.transpose(1, 0, 3, 2, 4).reshape(total, slab, width)
    logits_cols = error_logits(updated, mirrored, w_pae, w_pde)
    return lax.all_to_all(
        logits_cols.astype(jnp.bfloat16), "row", split_axis=0, concat_axis=1, tiled=True
    ).astype(logits_cols.dtype)


def solution(mesh):
    in_specs = (
        P("row", "col", None),
        P(None, ("row", "col")),
        P(("row", "col")),
        P(),
        P(),
        P(),
        P(),
        P(),
        P(),
    )
    out_specs = P("row", "col", None)
    return jax.shard_map(
        per_device, mesh=mesh, in_specs=in_specs, out_specs=out_specs, check_vma=False
    )
```

profile of v0, /device:TPU:1, one launch (start us, length us, event | category | flops | bytes accessed | tf_op | source)
XLA Modules:
  0.0 1159.6 jit_solution(17012444799415025751)
XLA Ops:
  6.5 305.9 %all-gather = s32[128,8,3]{1,2,0:T(4,128)S(1)} all-gather(s32[1,8,3]{1,2,0:T(4,128)} %bitcast.145), channel_id=1, replica_groups=mesh['row'=16,'col'=8] {'row','col'}, dimensions={0}, use_global_device_ids=true | all-gather | bytes 12384 | tf_op jit(solution)/shard_map/all_gather | solution.py:60
  317.2 44.9 %all_to_all.23 = bf16[64,128,128]{2,0,1:T(8,128)(2,1)S(1)} all-to-all(bf16[64,128,128]{2,0,1:T(8,128)(2,1)S(1)} %copy.130), channel_id=1, replica_groups=mesh['row'=16,'col'=8] {'row'}, dimensions={1} | all-to-all | bytes 4194304 | tf_op jit(solution)/shard_map/all_to_all | solution.py:85
  364.9 6.8 multiply_reduce_fusion.1
  376.9 3.3 fusion.28
  380.3 9.3 convolution_bitcast_fusion
  391.3 63.1 %all-reduce = s32[1024]{0:T(1024)S(1)} all-reduce(s32[1024]{0:T(1024)S(1)} %dynamic-update-slice), channel_id=1, replica_groups=mesh['row'=16,'col'=8] {'row','col'}, use_global_device_ids=true, to_apply=%add | all-reduce | flops 1024 | bytes 8192
  454.9 6.1 fusion.30
  461.0 8.0 fusion.48
  472.9 11.7 %reshape.172 = bf16[1024,8,4,32]{3,2,1,0:T(4,128)(2,1)} reshape(bf16[8192,128]{1,0:T(8,128)(2,1)} %get-tuple-element.162) | data formatting | bytes 4194304 | tf_op jit(solution)/shard_map/reshape | solution.py:95
  484.6 12.2 %copy.146 = bf16[8,1024,4,32]{1,3,2,0:T(8,128)(2,1)} copy(bf16[8,1024,4,32]{3,2,0,1:T(4,128)(2,1)} %bitcast.133) | data formatting | bytes 4194304 | tf_op jit(solution)/shard_map/while | solution.py:116
  496.8 6.1 reshape.173
  502.9 12.2 %copy.147 = bf16[8,1024,4,32]{1,3,2,0:T(8,128)(2,1)} copy(bf16[8,1024,4,32]{3,2,0,1:T(4,128)(2,1)} %bitcast.134) | data formatting | bytes 4194304 | tf_op jit(solution)/shard_map/while | solution.py:116
  517.7 6.1 reshape.171
  523.8 12.3 %copy.145 = bf16[8,1024,4,32]{1,3,2,0:T(8,128)(2,1)} copy(bf16[8,1024,4,32]{3,2,0,1:T(4,128)(2,1)} %bitcast.135) | data formatting | bytes 4194304 | tf_op jit(solution)/shard_map/while | solution.py:116
  536.0 172.7 %all-gather.3.cloned.1.call-done = f32[4,1024,1024]{1,0,2:T(4,128)} async-done(((f32[4,1024,8]{1,0,2:T(4,128)}), f32[4,1024,1024]{1,0,2:T(4,128)}) %all-gather.3.cloned.1.call-update) | async-done | bytes 16777232 | tf_op jit(solution)/shard_map/all_gather | solution.py:104
  708.7 17.7 %copy.144 = f32[4,1024,8,16,8]{1,4,3,2,0:T(8,128)} copy(f32[4,1024,8,16,8]{1,0,4,2,3:T(4,128)} %bitcast.138) | data formatting | bytes 33554432 | tf_op jit(solution)/shard_map/transpose | solution.py:107
  726.4 297.7 %while.21 = (s32[]{:T(128)}, f32[8,1024,4,32]{3,2,1,0:T(4,128)}, bf16[8,1024,4,32]{1,3,2,0:T(8,128)(2,1)}, bf16[8,1024,4,32]{1,3,2,0:T(8,128)(2,1)}, bf16[8,1024...) while((s32[]{:T(128)}, f32[8,1024,4,32]{3,2,1,0:T(4,128)}, ...), condition=%wide.region_9.10_spmd, body=%wide.region_4.9_spmd.sunk | while | flops 421531648 | bytes 23358848 | solution.py:116
  728.7 32.8 %while.22 = (s32[]{:T(128)}, f32[2,512,4,32]{1,3,2,0:T(8,128)S(1)}, s32[2]{0:T(128)S(1)}, bf16[1024,4,32]{0,2,1:T(8,128)(2,1)S(1)}, bf16[1024,4,32]{0,2,1:T(8,12...) while((s32[]{:T(128)}, f32[2,512,4,32]{1,3,2,0:T(8,128)S(1)}, ...), condition=%wide.region_8.8_spmd, body=%wide.region_5.7_spmd.sunk | while | flops 421531648 | bytes 18115228 | solution.py:40
  731.3 5.7 fusion.70
  736.9 8.2 fusion.71
  747.7 5.6 fusion.70
  753.3 8.1 fusion.71
  765.9 32.8 %while.22 = (s32[]{:T(128)}, f32[2,512,4,32]{1,3,2,0:T(8,128)S(1)}, s32[2]{0:T(128)S(1)}, bf16[1024,4,32]{0,2,1:T(8,128)(2,1)S(1)}, bf16[1024,4,32]{0,2,1:T(8,12...) while((s32[]{:T(128)}, f32[2,512,4,32]{1,3,2,0:T(8,128)S(1)}, ...), condition=%wide.region_8.8_spmd, body=%wide.region_5.7_spmd.sunk | while | flops 421531648 | bytes 18115228 | solution.py:40
  768.5 5.7 fusion.70
  774.1 8.2 fusion.71
  784.9 5.6 fusion.70
  790.5 8.1 fusion.71
  803.0 32.8 %while.22 = (s32[]{:T(128)}, f32[2,512,4,32]{1,3,2,0:T(8,128)S(1)}, s32[2]{0:T(128)S(1)}, bf16[1024,4,32]{0,2,1:T(8,128)(2,1)S(1)}, bf16[1024,4,32]{0,2,1:T(8,12...) while((s32[]{:T(128)}, f32[2,512,4,32]{1,3,2,0:T(8,128)S(1)}, ...), condition=%wide.region_8.8_spmd, body=%wide.region_5.7_spmd.sunk | while | flops 421531648 | bytes 18115228 | solution.py:40
  805.6 5.7 fusion.70
  811.3 8.2 fusion.71
  822.0 5.6 fusion.70
  827.7 8.1 fusion.71
  840.2 32.8 %while.22 = (s32[]{:T(128)}, f32[2,512,4,32]{1,3,2,0:T(8,128)S(1)}, s32[2]{0:T(128)S(1)}, bf16[1024,4,32]{0,2,1:T(8,128)(2,1)S(1)}, bf16[1024,4,32]{0,2,1:T(8,12...) while((s32[]{:T(128)}, f32[2,512,4,32]{1,3,2,0:T(8,128)S(1)}, ...), condition=%wide.region_8.8_spmd, body=%wide.region_5.7_spmd.sunk | while | flops 421531648 | bytes 18115228 | solution.py:40
  842.8 5.7 fusion.70
  848.5 8.2 fusion.71
  859.2 5.6 fusion.70
  864.9 8.1 fusion.71
  877.4 32.8 %while.22 = (s32[]{:T(128)}, f32[2,512,4,32]{1,3,2,0:T(8,128)S(1)}, s32[2]{0:T(128)S(1)}, bf16[1024,4,32]{0,2,1:T(8,128)(2,1)S(1)}, bf16[1024,4,32]{0,2,1:T(8,12...) while((s32[]{:T(128)}, f32[2,512,4,32]{1,3,2,0:T(8,128)S(1)}, ...), condition=%wide.region_8.8_spmd, body=%wide.region_5.7_spmd.sunk | while | flops 421531648 | bytes 18115228 | solution.py:40
  880.0 5.7 fusion.70
  885.7 8.2 fusion.71
  896.4 5.6 fusion.70
  902.1 8.1 fusion.71
  914.7 32.8 %while.22 = (s32[]{:T(128)}, f32[2,512,4,32]{1,3,2,0:T(8,128)S(1)}, s32[2]{0:T(128)S(1)}, bf16[1024,4,32]{0,2,1:T(8,128)(2,1)S(1)}, bf16[1024,4,32]{0,2,1:T(8,12...) while((s32[]{:T(128)}, f32[2,512,4,32]{1,3,2,0:T(8,128)S(1)}, ...), condition=%wide.region_8.8_spmd, body=%wide.region_5.7_spmd.sunk | while | flops 421531648 | bytes 18115228 | solution.py:40
  917.3 5.7 fusion.70
  922.9 8.2 fusion.71
  933.7 5.6 fusion.70
  939.3 8.1 fusion.71
  951.8 32.8 %while.22 = (s32[]{:T(128)}, f32[2,512,4,32]{1,3,2,0:T(8,128)S(1)}, s32[2]{0:T(128)S(1)}, bf16[1024,4,32]{0,2,1:T(8,128)(2,1)S(1)}, bf16[1024,4,32]{0,2,1:T(8,12...) while((s32[]{:T(128)}, f32[2,512,4,32]{1,3,2,0:T(8,128)S(1)}, ...), condition=%wide.region_8.8_spmd, body=%wide.region_5.7_spmd.sunk | while | flops 421531648 | bytes 18115228 | solution.py:40
  954.4 5.7 fusion.70
  960.1 8.2 fusion.71
  970.8 5.6 fusion.70
  976.4 8.1 fusion.71
  989.0 32.8 %while.22 = (s32[]{:T(128)}, f32[2,512,4,32]{1,3,2,0:T(8,128)S(1)}, s32[2]{0:T(128)S(1)}, bf16[1024,4,32]{0,2,1:T(8,128)(2,1)S(1)}, bf16[1024,4,32]{0,2,1:T(8,12...) while((s32[]{:T(128)}, f32[2,512,4,32]{1,3,2,0:T(8,128)S(1)}, ...), condition=%wide.region_8.8_spmd, body=%wide.region_5.7_spmd.sunk | while | flops 421531648 | bytes 18115228 | solution.py:40
  991.6 5.7 fusion.70
  997.3 8.2 fusion.71
  1008.0 5.7 fusion.70
  1013.7 8.1 fusion.71
  1024.2 15.3 %copy.148 = f32[1024,8,4,32]{3,2,1,0:T(4,128)} copy(f32[1024,8,4,32]{3,2,0,1:T(4,128)} %bitcast.139) | data formatting | bytes 8388608 | tf_op jit(solution)/shard_map/transpose | solution.py:120
  1039.5 13.5 %reshape.176 = f32[8192,128]{1,0:T(8,128)} reshape(f32[1024,8,4,32]{3,2,1,0:T(4,128)} %copy.148) | data formatting | bytes 8388608 | tf_op jit(solution)/shard_map/reshape | solution.py:120
  1052.9 5.6 convert_reduce_fusion
  1060.1 9.8 all-to-all-start.1
  1069.9 29.8 %all-to-all-done.1 = bf16[128,8,8,128]{3,2,1,0:T(8,128)(2,1)} async-done(((bf16[128,8,8,128]{3,2,1,0:T(8,128)(2,1)}), bf16[128,8,8,128]{3,2,1,0:T(8,128)(2,1)}, u32[]{:S(2)}, u32[]{:S(2)}) %all-to-all-start.1) | async-done | bytes 2097184 | tf_op jit(solution)/shard_map/all_to_all | solution.py:127
  1102.8 3.8 fusion.24
  1118.5 31.5 %all_to_all.24 = bf16[1024,8,128]{2,1,0:T(8,128)(2,1)S(1)} all-to-all(bf16[1024,8,128]{2,1,0:T(8,128)(2,1)} %bitcast.142), channel_id=1, replica_groups=mesh['row'=16,'col'=8] {'row'}, dimensions={0} | all-to-all | bytes 4194304 | tf_op jit(solution)/shard_map/all_to_all | solution.py:131
  (124 shorter events, 85.9 us)
Async XLA Ops:
  6.5 454.5 %copy-start = (bf16[128,512]{1,0:T(8,128)(2,1)S(1)}, bf16[128,512]{1,0:T(8,128)(2,1)}, u32[]{:S(2)}) copy-start(bf16[128,512]{1,0:T(8,128)(2,1)} %param.17) | copy-start | bytes 393220
  6.5 702.2 %all-gather.3.cloned.1.call-start = ((), (), s32[]{:S(2)}) async-start(), calls=%async_computation.3 | async-start | bytes 16908288 | tf_op jit(solution)/shard_map/all_gather | solution.py:104
  374.9 2.0 copy-start.2
  374.9 5.3 copy-start.5
  380.2 10.8 copy-start.8
  469.0 3.8 copy-start.3
  1039.5 13.5 %copy-start.6 = (bf16[128,128]{1,0:T(8,128)(2,1)S(1)}, bf16[128,128]{1,0:T(8,128)(2,1)}, u32[]{:S(2)}) copy-start(bf16[128,128]{1,0:T(8,128)(2,1)} %param.19) | copy-start | bytes 98308
  1060.1 39.7 %all-to-all-start.1 = ((bf16[128,8,8,128]{3,2,1,0:T(8,128)(2,1)}), bf16[128,8,8,128]{3,2,1,0:T(8,128)(2,1)}, u32[]{:S(2)}, u32[]{:S(2)}) async-start(bf16[128,8,8,128]{3,2,1,0:T(8,128)(2,1)} %bitcast.141), calls=%async_computation.1 | async-start | bytes 4194304 | tf_op jit(solution)/shard_map/all_to_all | solution.py:127
  1106.6 3.0 copy-start.7
  1106.6 6.1 copy-start.4
  1118.5 34.0 %copy-start.1 = (bf16[128,512]{1,0:T(8,128)(2,1)S(1)}, bf16[128,512]{1,0:T(8,128)(2,1)}, u32[]{:S(2)}) copy-start(bf16[128,512]{1,0:T(8,128)(2,1)} %param.17) | copy-start | bytes 393220
Sparse Core Ops, SparseCore 0:
  391.1 317.5 all-gather.2
where the time goes:
time: 1170 us; the launch traced here: 1160 us
  blocking collectives  445 us (38%)
  matrix products  253 us (22%)
  waiting for transfers between devices  203 us (17%)
  local copies, waits for them, and re-layouts  170 us (15%)
  other arithmetic  33.9 us (3%)
  loops' own time  31.2 us (3%)
  between operations  14 us (1%)
    all_gather x1, blocking collectives, per_device(): lax.all_gather(coords, ('row', 'col'), axis=1, tiled=True)  306 us
    all_gather x1, waiting for transfers between devices, per_device(): gathered = lax.all_gather(bias_local, ('row', 'col'), axis=2, tiled=True)  173 us
    dot_general x16, matrix products, one_block(): jnp.einsum('hki,khd->ihd', weights, value_rows, preferred_element_type=jn...  130 us
    sub x16, matrix products, one_block(): raised = jnp.exp(scores - highest)  90.4 us
    unnamed x1, blocking collectives  63.1 us
    all_to_all x1, blocking collectives, per_device(): lax.all_to_all(pair, 'row', split_axis=1, concat_axis=0, tiled=True)  44.9 us
    while x3, local copies, waits for them, and re-layouts, per_device(): lax.map(one_column, (jnp.swapaxes(query_all, 0, 1), jnp.swapaxes(key_all,...  36.7 us
    all_to_all x1, blocking collectives, per_device(): lax.all_to_all(logits_cols.astype(jnp.bfloat16), 'row', split_axis=0, con...  31.5 us
  transfers between devices with their start and end apart: 2, of which 2 were waited for; matrix products, arithmetic and copies ran while one was open for 7% of the time, Pallas kernels for 0%

commit v1 on v0

--- a/solution.py
+++ b/solution.py
@@ -101,7 +101,8 @@
     )
     gate_all = projected[:, 3 * width :].astype(jnp.bfloat16)
     bias_local = jnp.einsum("kic,ch->hki", normed, w_bias, preferred_element_type=jnp.float32)
-    gathered = lax.all_gather(bias_local, ("row", "col"), axis=2, tiled=True)
+    repeated = jnp.stack([bias_local] * lax.axis_size(("row", "col")))
+    gathered = jnp.concatenate(lax.all_to_all(repeated, ("row", "col"), 0, 0), axis=2)
     bias_full = (
         gathered.reshape(heads, total, n_rows, n_cols, slab)
         .transpose(0, 1, 3, 2, 4)

time: 1170 us -> 1210 us (1.034)
  blocking collectives: 445 us -> 674 us
  waiting for transfers between devices: 203 us -> 29.8 us
  between operations: 14 us -> 0.59 us
    unnamed x1, blocking collectives: 63.1 us -> 292 us
    all_gather x1 -> x0, waiting for transfers between devices: 173 us -> none  [per_device(): gathered = lax.all_gather(bias_local, ('row', 'col'), axis=2, tiled=True)]
  transfers between devices with their start and end apart: 2 -> 2, of which waited for: 2 -> 1; matrix products, arithmetic and copies ran while one was open for 7% -> 7% of each run, Pallas kernels for 0% -> 0%
where the time goes in v1:
time: 1210 us
  blocking collectives  674 us (56%)
  matrix products  253 us (21%)
  local copies, waits for them, and re-layouts  171 us (14%)
  other arithmetic  33.9 us (3%)
  loops' own time  31.2 us (3%)
  waiting for transfers between devices  29.8 us (2%)
  starting transfers between devices  12.3 us (1%)
    all_gather x1, blocking collectives, per_device(): lax.all_gather(coords, ('row', 'col'), axis=1, tiled=True)  306 us
    unnamed x1, blocking collectives  292 us
    dot_general x16, matrix products, one_block(): jnp.einsum('hki,khd->ihd', weights, value_rows, preferred_element_type=jn...  130 us
    sub x16, matrix products, one_block(): raised = jnp.exp(scores - highest)  90.6 us
    all_to_all x1, blocking collectives, per_device(): lax.all_to_all(pair, 'row', split_axis=1, concat_axis=0, tiled=True)  44.9 us
    while x3, local copies, waits for them, and re-layouts, per_device(): lax.map(one_column, (jnp.swapaxes(query_all, 0, 1), jnp.swapaxes(key_all,...  36.7 us
    all_to_all x1, blocking collectives, per_device(): lax.all_to_all(logits_cols.astype(jnp.bfloat16), 'row', split_axis=0, con...  31.5 us
    another operation x8, loops' own time, attend_column(): blocks_out = lax.map(one_block, starts)  30.7 us
  transfers between devices with their start and end apart: 2, of which 1 were waited for; matrix products, arithmetic and copies ran while one was open for 7% of the time, Pallas kernels for 0%

profile of v1, /device:TPU:1, one launch (start us, length us, event | category | flops | bytes accessed | tf_op | source)
XLA Modules:
  0.0 1205.4 jit_solution(2378054919660747114)
XLA Ops:
  0.0 305.9 %all-gather = s32[128,8,3]{1,2,0:T(4,128)S(1)} all-gather(s32[1,8,3]{1,2,0:T(4,128)} %bitcast.145), channel_id=1, replica_groups=mesh['row'=16,'col'=8] {'row','col'}, dimensions={0}, use_global_device_ids=true | all-gather | bytes 12384 | tf_op jit(solution)/shard_map/all_gather | solution.py:60
  310.7 44.9 %all_to_all.28 = bf16[64,128,128]{2,0,1:T(8,128)(2,1)S(1)} all-to-all(bf16[64,128,128]{2,0,1:T(8,128)(2,1)S(1)} %copy.154), channel_id=1, replica_groups=mesh['row'=16,'col'=8] {'row'}, dimensions={1} | all-to-all | bytes 4194304 | tf_op jit(solution)/shard_map/all_to_all | solution.py:85
  358.4 6.8 multiply_reduce_fusion.1
  373.7 9.3 convolution_bitcast_fusion
  383.9 7.9 stack.2
  391.8 6.1 all-to-all-start.1
  398.2 291.5 %all-reduce = s32[1024]{0:T(1024)S(1)} all-reduce(s32[1024]{0:T(1024)S(1)} %dynamic-update-slice), channel_id=1, replica_groups=mesh['row'=16,'col'=8] {'row','col'}, use_global_device_ids=true, to_apply=%add | all-reduce | flops 1024 | bytes 8192
  690.3 6.1 fusion.30
  696.4 8.0 fusion.48
  708.2 11.7 reshape.174
  719.9 12.2 %copy.171 = bf16[8,1024,4,32]{1,3,2,0:T(8,128)(2,1)} copy(bf16[8,1024,4,32]{3,2,0,1:T(4,128)(2,1)} %bitcast.134) | data formatting | bytes 4194304 | tf_op jit(solution)/shard_map/while | solution.py:117
  732.2 6.1 reshape.175
  738.3 12.2 %copy.172 = bf16[8,1024,4,32]{1,3,2,0:T(8,128)(2,1)} copy(bf16[8,1024,4,32]{3,2,0,1:T(4,128)(2,1)} %bitcast.135) | data formatting | bytes 4194304 | tf_op jit(solution)/shard_map/while | solution.py:117
  753.0 6.0 reshape.173
  759.0 12.2 %copy.170 = bf16[8,1024,4,32]{1,3,2,0:T(8,128)(2,1)} copy(bf16[8,1024,4,32]{3,2,0,1:T(4,128)(2,1)} %bitcast.136) | data formatting | bytes 4194304 | tf_op jit(solution)/shard_map/while | solution.py:117
  771.3 11.8 copy.169
  783.1 297.3 %while.21 = (s32[]{:T(128)}, f32[8,1024,4,32]{3,2,1,0:T(4,128)}, bf16[8,1024,4,32]{1,3,2,0:T(8,128)(2,1)}, bf16[8,1024,4,32]{1,3,2,0:T(8,128)(2,1)}, bf16[8,1024...) while((s32[]{:T(128)}, f32[8,1024,4,32]{3,2,1,0:T(4,128)}, ...), condition=%wide.region_9.10_spmd, body=%wide.region_4.9_spmd.sunk | while | flops 421531648 | bytes 23358848 | solution.py:117
  785.3 32.7 %while.22 = (s32[]{:T(128)}, f32[2,512,4,32]{1,3,2,0:T(8,128)S(1)}, s32[2]{0:T(128)S(1)}, bf16[1024,4,32]{0,2,1:T(8,128)(2,1)S(1)}, bf16[1024,4,32]{0,2,1:T(8,12...) while((s32[]{:T(128)}, f32[2,512,4,32]{1,3,2,0:T(8,128)S(1)}, ...), condition=%wide.region_8.8_spmd, body=%wide.region_5.7_spmd.sunk | while | flops 421531648 | bytes 18115228 | solution.py:40
  787.9 5.7 fusion.70
  793.6 8.2 fusion.71
  804.3 5.7 fusion.70
  809.9 8.1 fusion.71
  822.5 32.7 %while.22 = (s32[]{:T(128)}, f32[2,512,4,32]{1,3,2,0:T(8,128)S(1)}, s32[2]{0:T(128)S(1)}, bf16[1024,4,32]{0,2,1:T(8,128)(2,1)S(1)}, bf16[1024,4,32]{0,2,1:T(8,12...) while((s32[]{:T(128)}, f32[2,512,4,32]{1,3,2,0:T(8,128)S(1)}, ...), condition=%wide.region_8.8_spmd, body=%wide.region_5.7_spmd.sunk | while | flops 421531648 | bytes 18115228 | solution.py:40
  825.0 5.7 fusion.70
  830.7 8.2 fusion.71
  841.4 5.7 fusion.70
  847.1 8.1 fusion.71
  859.6 32.7 %while.22 = (s32[]{:T(128)}, f32[2,512,4,32]{1,3,2,0:T(8,128)S(1)}, s32[2]{0:T(128)S(1)}, bf16[1024,4,32]{0,2,1:T(8,128)(2,1)S(1)}, bf16[1024,4,32]{0,2,1:T(8,12...) while((s32[]{:T(128)}, f32[2,512,4,32]{1,3,2,0:T(8,128)S(1)}, ...), condition=%wide.region_8.8_spmd, body=%wide.region_5.7_spmd.sunk | while | flops 421531648 | bytes 18115228 | solution.py:40
  862.1 5.7 fusion.70
  867.8 8.2 fusion.71
  878.5 5.6 fusion.70
  884.1 8.1 fusion.71
  896.7 32.7 %while.22 = (s32[]{:T(128)}, f32[2,512,4,32]{1,3,2,0:T(8,128)S(1)}, s32[2]{0:T(128)S(1)}, bf16[1024,4,32]{0,2,1:T(8,128)(2,1)S(1)}, bf16[1024,4,32]{0,2,1:T(8,12...) while((s32[]{:T(128)}, f32[2,512,4,32]{1,3,2,0:T(8,128)S(1)}, ...), condition=%wide.region_8.8_spmd, body=%wide.region_5.7_spmd.sunk | while | flops 421531648 | bytes 18115228 | solution.py:40
  899.2 5.7 fusion.70
  904.9 8.2 fusion.71
  915.6 5.7 fusion.70
  921.3 8.1 fusion.71
  933.8 32.7 %while.22 = (s32[]{:T(128)}, f32[2,512,4,32]{1,3,2,0:T(8,128)S(1)}, s32[2]{0:T(128)S(1)}, bf16[1024,4,32]{0,2,1:T(8,128)(2,1)S(1)}, bf16[1024,4,32]{0,2,1:T(8,12...) while((s32[]{:T(128)}, f32[2,512,4,32]{1,3,2,0:T(8,128)S(1)}, ...), condition=%wide.region_8.8_spmd, body=%wide.region_5.7_spmd.sunk | while | flops 421531648 | bytes 18115228 | solution.py:40
  936.4 5.7 fusion.70
  942.1 8.2 fusion.71
  952.8 5.7 fusion.70
  958.4 8.1 fusion.71
  971.0 32.7 %while.22 = (s32[]{:T(128)}, f32[2,512,4,32]{1,3,2,0:T(8,128)S(1)}, s32[2]{0:T(128)S(1)}, bf16[1024,4,32]{0,2,1:T(8,128)(2,1)S(1)}, bf16[1024,4,32]{0,2,1:T(8,12...) while((s32[]{:T(128)}, f32[2,512,4,32]{1,3,2,0:T(8,128)S(1)}, ...), condition=%wide.region_8.8_spmd, body=%wide.region_5.7_spmd.sunk | while | flops 421531648 | bytes 18115228 | solution.py:40
  973.6 5.7 fusion.70
  979.3 8.2 fusion.71
  990.0 5.7 fusion.70
  995.6 8.1 fusion.71
  1008.2 32.7 %while.22 = (s32[]{:T(128)}, f32[2,512,4,32]{1,3,2,0:T(8,128)S(1)}, s32[2]{0:T(128)S(1)}, bf16[1024,4,32]{0,2,1:T(8,128)(2,1)S(1)}, bf16[1024,4,32]{0,2,1:T(8,12...) while((s32[]{:T(128)}, f32[2,512,4,32]{1,3,2,0:T(8,128)S(1)}, ...), condition=%wide.region_8.8_spmd, body=%wide.region_5.7_spmd.sunk | while | flops 421531648 | bytes 18115228 | solution.py:40
  1010.7 5.7 fusion.70
  1016.4 8.2 fusion.71
  1027.1 5.7 fusion.70
  1032.7 8.1 fusion.71
  1045.3 32.7 %while.22 = (s32[]{:T(128)}, f32[2,512,4,32]{1,3,2,0:T(8,128)S(1)}, s32[2]{0:T(128)S(1)}, bf16[1024,4,32]{0,2,1:T(8,128)(2,1)S(1)}, bf16[1024,4,32]{0,2,1:T(8,12...) while((s32[]{:T(128)}, f32[2,512,4,32]{1,3,2,0:T(8,128)S(1)}, ...), condition=%wide.region_8.8_spmd, body=%wide.region_5.7_spmd.sunk | while | flops 421531648 | bytes 18115228 | solution.py:40
  1047.8 5.7 fusion.70
  1053.5 8.2 fusion.71
  1064.2 5.6 fusion.70
  1069.9 8.1 fusion.71
  1080.3 15.3 %copy.173 = f32[1024,8,4,32]{3,2,1,0:T(4,128)} copy(f32[1024,8,4,32]{3,2,0,1:T(4,128)} %bitcast.139) | data formatting | bytes 8388608 | tf_op jit(solution)/shard_map/transpose | solution.py:121
  1095.6 13.5 %reshape.178 = f32[8192,128]{1,0:T(8,128)} reshape(f32[1024,8,4,32]{3,2,1,0:T(4,128)} %copy.173) | data formatting | bytes 8388608 | tf_op jit(solution)/shard_map/reshape | solution.py:121
  1109.1 5.6 convert_reduce_fusion
  1116.3 6.2 all-to-all-start.2
  1122.5 29.8 %all-to-all-done.2 = bf16[128,8,8,128]{3,2,1,0:T(8,128)(2,1)} async-done(((bf16[128,8,8,128]{3,2,1,0:T(8,128)(2,1)}), bf16[128,8,8,128]{3,2,1,0:T(8,128)(2,1)}, u32[]{:S(2)}, u32[]{:S(2)}) %all-to-all-start.2) | async-done | bytes 2097184 | tf_op jit(solution)/shard_map/all_to_all | solution.py:128
  1155.4 3.8 fusion.24
  1171.0 31.5 %all_to_all.29 = bf16[1024,8,128]{2,1,0:T(8,128)(2,1)S(1)} all-to-all(bf16[1024,8,128]{2,1,0:T(8,128)(2,1)} %bitcast.142), channel_id=1, replica_groups=mesh['row'=16,'col'=8] {'row'}, dimensions={0} | all-to-all | bytes 4194304 | tf_op jit(solution)/shard_map/all_to_all | solution.py:132
  (124 shorter events, 88.1 us)
Async XLA Ops:
  0.0 696.4 %copy-start = (bf16[128,512]{1,0:T(8,128)(2,1)S(1)}, bf16[128,512]{1,0:T(8,128)(2,1)}, u32[]{:S(2)}) copy-start(bf16[128,512]{1,0:T(8,128)(2,1)} %param.17) | copy-start | bytes 393220
  368.4 2.0 copy-start.2
  368.4 5.3 copy-start.5
  391.8 6.2 copy-start.8
  391.8 379.5 %all-to-all-start.1 = ((f32[128,4,1024,8]{2,3,1,0:T(8,128)}), f32[128,4,1024,8]{2,3,1,0:T(8,128)}, u32[]{:S(2)}, u32[]{:S(2)}) async-start(f32[128,4,1024,8]{2,3,1,0:T(8,128)} %stack.2), calls=%async_computation.1 | async-start | bytes 33554432 | tf_op jit(solution)/shard_map/all_to_all | solution.py:105
  704.4 3.8 copy-start.3
  1095.6 13.5 %copy-start.6 = (bf16[128,128]{1,0:T(8,128)(2,1)S(1)}, bf16[128,128]{1,0:T(8,128)(2,1)}, u32[]{:S(2)}) copy-start(bf16[128,128]{1,0:T(8,128)(2,1)} %param.19) | copy-start | bytes 98308
  1116.3 36.0 %all-to-all-start.2 = ((bf16[128,8,8,128]{3,2,1,0:T(8,128)(2,1)}), bf16[128,8,8,128]{3,2,1,0:T(8,128)(2,1)}, u32[]{:S(2)}, u32[]{:S(2)}) async-start(bf16[128,8,8,128]{3,2,1,0:T(8,128)(2,1)} %bitcast.141), calls=%async_computation.2 | async-start | bytes 4194304 | tf_op jit(solution)/shard_map/all_to_all | solution.py:128
  1159.2 3.0 copy-start.7
  1159.2 6.1 copy-start.4
  1171.0 34.0 %copy-start.1 = (bf16[128,512]{1,0:T(8,128)(2,1)S(1)}, bf16[128,512]{1,0:T(8,128)(2,1)}, u32[]{:S(2)}) copy-start(bf16[128,512]{1,0:T(8,128)(2,1)} %param.17) | copy-start | bytes 393220
